TPU v7x, 256 devices: a whole 4x4x8 slice. The times are simulated.
256 devices in a mesh: ctx: 64 (over z, y, core), ch: 4 (over x).
Axes of the slice: x: 4, y: 4, z: 8, core: 2. Of those that a mesh axis runs over, the one named last changes fastest.
Arguments:
- conv_input: bfloat16 [256, 128, 8192], P('ctx', None, 'ch'), may hold values from -6 to 6
- gate_signal: bfloat16 [256, 128, 8192], P('ctx', None, 'ch'), may hold values from -6 to 6
- cotangent: bfloat16 [256, 128, 8192], P('ctx', None, 'ch'), may hold values from -6 to 6
- filters: float32 [16, 1024], replicated
- tile_owner: int32 [192], replicated, may hold values from 0 to 63, as said below
- support: int32 [192, 8], replicated, may hold values from -1 to 191, as said below
Outputs:
- gate_grad: bfloat16 [256, 128, 8192], P('ctx', None, 'ch')
- input_grad: bfloat16 [256, 128, 8192], P('ctx', None, 'ch')
- filter_grad: float32 [16, 1024], replicated
Inputs may be any that keep to these rules, and one draw needn't show every extreme that they name: tile_owner never falls from one tile to the next; every index of ctx owns from 2 to 4 tiles, some index owns 3 + 1 and some index owns 3 - 1. support[t, k] is t - k where tile t - k belongs to the document of tile t and -1 otherwise; documents are runs of whole tiles, and some document spans 8 tiles or more.
All inputs are finite; a program needn't handle non-finite values.
Results may differ from a plain program's by a relative error of at most 0.0058.
Values may be sent and summed in bfloat16 or wider, within the bound.
No kernel may reach another device: no remote copies, remote signals or barrier semaphores. Data moves between devices by JAX's collectives and lax.ppermute only.
A program may use at most 256 MiB of HBM per device.

v0:
```python
import math
import jax
import jax.numpy as jnp
from jax import lax
from jax.sharding import PartitionSpec as P

GROUP = 128
REACH = 4


def passed_along(value, axis, steps):
    count = lax.axis_size(axis)
    leading, last = (max(0, -steps), min(count, count - steps))
    return lax.ppermute(value, axis, [(source, source + steps) for source in range(leading, last)])


def filter_blocks(filters, tile_rows, maxlag):
    narrow = filters.astype(jnp.bfloat16)
    row_ids = jnp.arange(tile_rows, dtype=jnp.int32)
    lag_offsets = (
        jnp.arange(maxlag, dtype=jnp.int32)[:, None, None] * tile_rows
        + row_ids[:, None]
        - row_ids[None, :]
    )
    picked = jnp.take(narrow, jnp.clip(lag_offsets, 0, filters.shape[1] - 1), axis=1)
    return jnp.where(lag_offsets[None] >= 0, picked, jnp.zeros_like(picked))


def lag_sums(square):
    filter_count, side_length = (square.shape[0], square.shape[1])
    flipped = square[:, :, ::-1]
    padded = jnp.pad(flipped, ((0, 0), (0, 0), (0, side_length)))
    skewed = padded.reshape(filter_count, 2 * side_length * side_length)[
        :, : side_length * (2 * side_length - 1)
    ]
    return jnp.sum(skewed.reshape(filter_count, side_length, 2 * side_length - 1), axis=1)


def spread_lags(squares, lag_count):
    maxlag, filter_count, side_length = (squares.shape[0], squares.shape[1], squares.shape[2])
    accumulated = jnp.zeros((filter_count, (maxlag + 1) * side_length), jnp.float32)
    for lag_index in range(maxlag):
        start_col = lag_index * side_length
        accumulated = accumulated.at[:, start_col : start_col + 2 * side_length - 1].add(
            lag_sums(squares[lag_index])
        )
    return accumulated[:, side_length - 1 : side_length - 1 + lag_count]


def per_device(conv_input, gate_signal, cotangent, filters, tile_owner, support):
    slot_count, tile_rows, channels = conv_input.shape
    maxlag = support.shape[1]
    filter_count, lag_count = filters.shape
    group_width = GROUP
    repeats = channels // (filter_count * group_width)
    total_tiles = tile_owner.shape[0]
    devices_ctx = lax.axis_size("ctx")
    myself = lax.axis_index("ctx")
    farthest = REACH
    devices = jnp.arange(devices_ctx, dtype=jnp.int32)
    counts = jnp.sum((tile_owner[None, :] == devices[:, None]).astype(jnp.int32), axis=1)
    starts = jnp.cumsum(counts) - counts
    slot_index = jnp.arange(slot_count, dtype=jnp.int32)
    own_tiles = starts[myself] + slot_index
    own_live = slot_index < counts[myself]
    own_safe = jnp.clip(own_tiles, 0, total_tiles - 1)
    sources = support[own_safe]
    present = own_live[:, None] & (sources >= 0)
    source_safe = jnp.clip(sources, 0, total_tiles - 1)
    holder = tile_owner[source_safe]
    within = source_safe - starts[holder]
    blocks = filter_blocks(filters, tile_rows, maxlag)
    zero_tile = jnp.zeros((), jnp.bfloat16)
    gathered = [conv_input]
    for distance in range(1, farthest + 1):
        gathered.append(passed_along(conv_input, "ctx", distance))
    window = jnp.concatenate(gathered, axis=0)
    rows_at = jnp.clip((myself - holder) * slot_count + within, 0, window.shape[0] - 1)
    selected = jnp.take(window, rows_at.reshape(-1), axis=0)
    selected = selected.reshape(slot_count, maxlag, tile_rows, channels)
    selected = jnp.where(present[:, :, None, None], selected, zero_tile)
    weighted = (gate_signal.astype(jnp.float32) * cotangent.astype(jnp.float32)).astype(
        jnp.bfloat16
    )
    weighted = jnp.where(own_live[:, None, None], weighted, zero_tile)
    weighted_shaped = weighted.reshape(slot_count, tile_rows, repeats, filter_count, group_width)
    conv_out = jnp.zeros((slot_count, tile_rows, channels), jnp.float32)
    squares = []
    for lag_index in range(maxlag):
        shaped = selected[:, lag_index].reshape(
            slot_count, tile_rows, repeats, filter_count, group_width
        )
        product = jnp.einsum(
            "fij,sjrfc->sirfc", blocks[:, lag_index], shaped, preferred_element_type=jnp.float32
        )
        conv_out = conv_out + product.reshape(slot_count, tile_rows, channels)
        squares.append(
            jnp.einsum(
                "sirfc,sjrfc->fij", weighted_shaped, shaped, preferred_element_type=jnp.float32
            )
        )
    gate_grad = (cotangent.astype(jnp.float32) * conv_out).astype(jnp.bfloat16)
    norm_factor = 1.0 / math.sqrt(
        total_tiles * tile_rows * channels * lax.axis_size("ch") / filter_count
    )
    local_filters = spread_lags(jnp.stack(squares), lag_count)
    filter_grad = lax.psum(local_filters, ("ctx", "ch")) * norm_factor
    row_count = (farthest + 1) * slot_count
    partial_value = jnp.zeros((row_count, tile_rows, channels), jnp.float32)
    back_rows = jnp.clip((myself - holder) * slot_count + within, 0, row_count - 1)
    for lag_index in range(maxlag):
        adjoint_term = jnp.einsum(
            "fji,sjrfc->sirfc",
            blocks[:, lag_index],
            weighted_shaped,
            preferred_element_type=jnp.float32,
        )
        adjoint_term = jnp.where(present[:, lag_index, None, None, None, None], adjoint_term, 0.0)
        partial_value = partial_value.at[back_rows[:, lag_index]].add(
            adjoint_term.reshape(slot_count, tile_rows, channels)
        )
    adjoint = partial_value[:slot_count]
    for distance in range(1, farthest + 1):
        adjoint = adjoint + passed_along(
            partial_value[distance * slot_count : (distance + 1) * slot_count], "ctx", -distance
        )
    input_grad = adjoint.astype(jnp.bfloat16)
    return (gate_grad, input_grad, filter_grad)


def solution(mesh):
    return jax.shard_map(
        per_device,
        mesh=mesh,
        in_specs=(P("ctx", None, "ch"), P("ctx", None, "ch"), P("ctx", None, "ch"), P(), P(), P()),
        out_specs=(P("ctx", None, "ch"), P("ctx", None, "ch"), P()),
        check_vma=False,
    )
```

profile of v0, /device:TPU:1, one launch (start us, length us, event | category | flops | bytes accessed | tf_op | source)
XLA Modules:
  0.0 1289.1 jit_solution(6269767289445348876)
XLA Ops:
  32.1 454.0 %gather_fusion.4 = bf16[131072,16]{1,0:T(8,128)(2,1)} fusion(bf16[16,1024]{0,1:T(8,128)(2,1)S(1)} %copy.164, s32[131072]{0:T(1024)S(1)} %broadcast_clamp_fusion), kind=kCustom, calls=%fused_computation.4 | custom fusion | bytes 8912896 | tf_op jit(solution)/shard_map/jit(_take)/gather | solution.py:25
  486.1 29.2 %copy.166 = bf16[8,128,128,16]{2,1,3,0:T(8,128)(2,1)} copy(bf16[8,128,128,16]{3,2,1,0:T(8,128)(2,1)} %bitcast.207) | data formatting | bytes 8388608 | tf_op jit(solution)/shard_map/jit(_take)/gather | solution.py:25
  547.7 5.4 copy.186
  553.1 4.7 copy.188
  557.7 5.4 copy.189
  563.1 4.7 copy.191
  567.8 5.4 copy.192
  573.2 4.7 copy.194
  577.8 5.4 copy.195
  583.2 4.7 copy.197
  587.9 5.4 copy.198
  593.3 4.7 copy.200
  598.0 5.6 copy.201
  603.5 4.7 copy.203
  608.2 5.4 copy.204
  618.2 5.4 copy.207
  623.9 9.7 broadcast_in_dim.155
  633.6 9.0 scatter_fusion
  642.5 9.0 scatter_fusion.1
  651.6 9.0 scatter_fusion.2
  660.6 9.0 scatter_fusion.3
  669.6 8.7 scatter_fusion.4
  678.3 8.6 scatter_fusion.5
  686.9 8.3 scatter_fusion.6
  695.1 8.3 scatter_fusion.7
  703.4 12.2 fusion.52
  742.8 11.4 gather_fusion.3
  754.2 8.7 select_select_fusion
  762.9 5.9 fusion.53
  836.1 11.8 add_bitcast_fusion
  850.1 9.3 rev.24
  863.5 6.2 reshape.668
  872.1 9.3 rev.25
  885.6 6.2 reshape.670
  893.5 6.0 rev.26
  903.6 6.2 reshape.672
  913.9 5.8 rev.27
  923.8 6.2 reshape.674
  934.1 6.0 rev.28
  944.3 6.2 reshape.676
  954.6 5.8 rev.29
  964.5 6.2 reshape.678
  974.8 6.1 rev.30
  985.0 6.2 reshape.680
  995.3 5.8 rev.31
  1005.2 6.3 reshape.682
  1028.9 241.1 %all-reduce.11.cloned.1.call-done = f32[16,1024]{1,0:T(8,128)} async-done(((f32[16,1024]{1,0:T(8,128)}), f32[16,1024]{1,0:T(8,128)}) %all-reduce.11.cloned.1.call-update) | async-done | bytes 65552 | tf_op jit(solution)/shard_map/psum | solution.py:107
  1271.5 10.4 fusion.5
  (174 shorter events, 234.9 us)
Async XLA Ops:
  7.2 24.7 %copy-start.7 = (f32[16,1024]{1,0:T(8,128)S(1)}, f32[16,1024]{1,0:T(8,128)}, u32[]{:S(2)}) copy-start(f32[16,1024]{1,0:T(8,128)} %param.25) | copy-start | bytes 196612
  7.2 1262.8 %all-reduce.11.cloned.1.call-start = ((), (), s32[]{:S(2)}) async-start(), calls=%async_computation | async-start | bytes 131072 | tf_op jit(solution)/shard_map/psum | solution.py:107
  7.2 718.4 %collective-permute-start = (bf16[4,128,2048]{2,1,0:T(8,128)(2,1)}, bf16[4,128,2048]{2,1,0:T(8,128)(2,1)}, u32[]{:S(2)}, u32[]{:S(2)}) collective-permute-start(bf16[4,128,2048]{2,1,0:T(8,128)(2,1)} %param.22), channel_id=1, source_target_pairs={{0,4},{4,8},{8,12},{12,16},{16,20},{20,24},{24,28},{28,32},{32,36}... | collective-permute-start | bytes 6291464 | tf_op jit(solution)/shard_map/ppermute | solution.py:14
  11.8 718.2 %collective-permute-start.1 = (bf16[4,128,2048]{2,1,0:T(8,128)(2,1)}, bf16[4,128,2048]{2,1,0:T(8,128)(2,1)}, u32[]{:S(2)}, u32[]{:S(2)}) collective-permute-start(bf16[4,128,2048]{2,1,0:T(8,128)(2,1)} %param.22), channel_id=1, source_target_pairs={{0,8},{4,12},{8,16},{12,20},{16,24},{20,28},{24,32},{28,36},{32,40... | collective-permute-start | bytes 6291464 | tf_op jit(solution)/shard_map/ppermute | solution.py:14
  16.3 718.2 %collective-permute-start.2 = (bf16[4,128,2048]{2,1,0:T(8,128)(2,1)}, bf16[4,128,2048]{2,1,0:T(8,128)(2,1)}, u32[]{:S(2)}, u32[]{:S(2)}) collective-permute-start(bf16[4,128,2048]{2,1,0:T(8,128)(2,1)} %param.22), channel_id=1, source_target_pairs={{0,12},{4,16},{8,20},{12,24},{16,28},{20,32},{24,36},{28,40},{32,4... | collective-permute-start | bytes 6291464 | tf_op jit(solution)/shard_map/ppermute | solution.py:14
  19.9 719.7 %collective-permute-start.3 = (bf16[4,128,2048]{2,1,0:T(8,128)(2,1)}, bf16[4,128,2048]{2,1,0:T(8,128)(2,1)}, u32[]{:S(2)}, u32[]{:S(2)}) collective-permute-start(bf16[4,128,2048]{2,1,0:T(8,128)(2,1)} %param.22), channel_id=1, source_target_pairs={{0,16},{4,20},{8,24},{12,28},{16,32},{20,36},{24,40},{28,44},{32,4... | collective-permute-start | bytes 6291464 | tf_op jit(solution)/shard_map/ppermute | solution.py:14
  486.1 29.2 %copy-start.6 = (bf16[4,128,2048]{2,1,0:T(8,128)(2,1)S(1)}, bf16[4,128,2048]{2,1,0:T(8,128)(2,1)}, u32[]{:S(2)}) copy-start(bf16[4,128,2048]{2,1,0:T(8,128)(2,1)} %param.24) | copy-start | bytes 6291460
  522.1 3.4 copy-start.5
  526.1 16.7 %copy-start = (bf16[16,8,128,128]{3,2,0,1:T(8,128)(2,1)}, bf16[16,8,128,128]{3,2,0,1:T(8,128)(2,1)S(1)}, u32[]{:S(2)}) copy-start(bf16[16,8,128,128]{3,2,0,1:T(8,128)(2,1)S(1)} %select_bitcast_fusion) | copy-start | bytes 12582916
  715.7 555.8 %collective-permute-start.7 = (f32[4,128,2048]{2,1,0:T(8,128)}, f32[4,128,2048]{2,1,0:T(8,128)}, u32[]{:S(2)}, u32[]{:S(2)}) collective-permute-start(f32[4,128,2048]{2,1,0:T(8,128)} %get-tuple-element.127), channel_id=1, source_target_pairs={{16,0},{20,4},{24,8},{28,12},{32,16},{36,20},{40,24},{44,28},{48,3... | collective-permute-start | bytes 12582920 | tf_op jit(solution)/shard_map/ppermute | solution.py:14
  725.6 545.8 %collective-permute-start.6 = (f32[4,128,2048]{2,1,0:T(8,128)}, f32[4,128,2048]{2,1,0:T(8,128)}, u32[]{:S(2)}, u32[]{:S(2)}) collective-permute-start(f32[4,128,2048]{2,1,0:T(8,128)} %get-tuple-element.128), channel_id=1, source_target_pairs={{12,0},{16,4},{20,8},{24,12},{28,16},{32,20},{36,24},{40,28},{44,3... | collective-permute-start | bytes 12582920 | tf_op jit(solution)/shard_map/ppermute | solution.py:14
  730.0 541.4 %collective-permute-start.5 = (f32[4,128,2048]{2,1,0:T(8,128)}, f32[4,128,2048]{2,1,0:T(8,128)}, u32[]{:S(2)}, u32[]{:S(2)}) collective-permute-start(f32[4,128,2048]{2,1,0:T(8,128)} %get-tuple-element.129), channel_id=1, source_target_pairs={{8,0},{12,4},{16,8},{20,12},{24,16},{28,20},{32,24},{36,28},{40,32... | collective-permute-start | bytes 12582920 | tf_op jit(solution)/shard_map/ppermute | solution.py:14
  734.5 536.9 %collective-permute-start.4 = (f32[4,128,2048]{2,1,0:T(8,128)}, f32[4,128,2048]{2,1,0:T(8,128)}, u32[]{:S(2)}, u32[]{:S(2)}) collective-permute-start(f32[4,128,2048]{2,1,0:T(8,128)} %get-tuple-element.126), channel_id=1, source_target_pairs={{4,0},{8,4},{12,8},{16,12},{20,16},{24,20},{28,24},{32,28},{36,32}... | collective-permute-start | bytes 12582920 | tf_op jit(solution)/shard_map/ppermute | solution.py:14
  772.8 4.5 copy-start.2
  783.0 4.5 copy-start.3
  793.2 4.5 copy-start.4
  1005.2 15.8 %copy-start.1 = (bf16[4,128,2048]{1,2,0:T(8,128)(2,1)S(1)}, bf16[4,128,2048]{1,2,0:T(8,128)(2,1)}, u32[]{:S(2)}) copy-start(bf16[4,128,2048]{1,2,0:T(8,128)(2,1)} %copy.160) | copy-start | bytes 6291460
Sparse Core Ops, SparseCore 0:
  1021.1 248.8 all-reduce.10
where the time goes:
time: 1300 us; the launch traced here: 1290 us
  local copies, waits for them, and re-layouts  807 us (62%)
  waiting for transfers between devices  241 us (19%)
  other arithmetic  126 us (10%)
  matrix products  78 us (6%)
  starting transfers between devices  22.1 us (2%)
  between operations  15.1 us (1%)
    gather x2, local copies, waits for them, and re-layouts, filter_blocks(): jnp.take(narrow, jnp.clip(lag_offsets, 0, filters.shape[1] - 1), axis=1)  483 us
    psum x1, waiting for transfers between devices, per_device(): filter_grad = lax.psum(local_filters, ('ctx', 'ch')) * norm_factor  241 us
    scatter-add x8, other arithmetic, per_device(): partial_value.at[back_rows[:, lag_index]]  69.9 us
    rev x8, local copies, waits for them, and re-layouts, lag_sums(): flipped = square[:, :, ::-1]  54.3 us
    reshape x8, local copies, waits for them, and re-layouts, lag_sums(): skewed.reshape(filter_count, side_length, 2 * side_length - 1)  49.4 us
    reshape x8, local copies, waits for them, and re-layouts, per_device(): adjoint_term.reshape(slot_count, tile_rows, channels)  43.4 us
    dot_general x8, matrix products, per_device(): jnp.einsum('fij,sjrfc->sirfc', blocks[:, lag_index], shaped, preferred_el...  42.7 us
    slice x9, local copies, waits for them, and re-layouts, per_device(): selected[:, lag_index]  37.9 us
  transfers between devices with their start and end apart: 9, of which 1 were waited for; matrix products, arithmetic and copies ran while one was open for 78% of the time, Pallas kernels for 0%

commit v1 on v0

--- a/solution.py
+++ b/solution.py
@@ -104,7 +104,7 @@
         total_tiles * tile_rows * channels * lax.axis_size("ch") / filter_count
     )
     local_filters = spread_lags(jnp.stack(squares), lag_count)
-    filter_grad = lax.psum(local_filters, ("ctx", "ch")) * norm_factor
+    filter_grad = jnp.sum(lax.all_gather(local_filters, ("ctx", "ch")), axis=0) * norm_factor
     row_count = (farthest + 1) * slot_count
     partial_value = jnp.zeros((row_count, tile_rows, channels), jnp.float32)
     back_rows = jnp.clip((myself - holder) * slot_count + within, 0, row_count - 1)

time: 1300 us -> 1470 us (1.13)
  the two profiles are of different devices: /device:TPU:1 before, /device:TPU:99 now
where the time goes in v1:
time: 1470 us; the launch traced here: 1460 us
  local copies, waits for them, and re-layouts  779 us (53%)
  waiting for transfers between devices  383 us (26%)
  other arithmetic  131 us (9%)
  starting transfers between devices  87.1 us (6%)
  matrix products  61.5 us (4%)
  between operations  15.1 us (1%)
    gather x2, local copies, waits for them, and re-layouts, filter_blocks(): jnp.take(narrow, jnp.clip(lag_offsets, 0, filters.shape[1] - 1), axis=1)  483 us
    ppermute x8, waiting for transfers between devices, passed_along(): lax.ppermute(value, axis, [(source, source + steps) for source in range(l...  383 us
    ppermute x8, starting transfers between devices, passed_along(): lax.ppermute(value, axis, [(source, source + steps) for source in range(l...  87 us
    scatter-add x8, other arithmetic, per_device(): partial_value.at[back_rows[:, lag_index]]  70.8 us
    reshape x8, local copies, waits for them, and re-layouts, lag_sums(): skewed.reshape(filter_count, side_length, 2 * side_length - 1)  49.2 us
    rev x8, local copies, waits for them, and re-layouts, lag_sums(): flipped = square[:, :, ::-1]  47.9 us
    reshape x8, local copies, waits for them, and re-layouts, per_device(): adjoint_term.reshape(slot_count, tile_rows, channels)  43.3 us
    slice x9, local copies, waits for them, and re-layouts, per_device(): selected[:, lag_index]  37.5 us
  transfers between devices with their start and end apart: 9, of which 6 were waited for; matrix products, arithmetic and copies ran while one was open for 50% of the time, Pallas kernels for 0%

profile of v1, /device:TPU:99, one launch (start us, length us, event | category | flops | bytes accessed | tf_op | source)
XLA Modules:
  0.0 1456.9 jit_solution(13110668147050535586)
XLA Ops:
  45.3 9.0 collective-permute-done
  57.4 111.9 %collective-permute-done.1 = bf16[4,128,2048]{2,1,0:T(8,128)(2,1)} collective-permute-done((bf16[4,128,2048]{2,1,0:T(8,128)(2,1)}, bf16[4,128,2048]{2,1,0:T(8,128)(2,1)}, u32[]{:S(2)}, u32[]{:S(2)}) %collective-permute-start.1) | collective-permute-done | bytes 2097184 | tf_op jit(solution)/shard_map/ppermute | solution.py:14
  180.9 11.1 gather_fusion.3
  192.0 8.7 select_select_fusion
  200.7 5.9 fusion.53
  240.5 5.8 rev.24
  250.5 6.2 reshape.668
  261.5 6.3 rev.25
  271.9 6.2 reshape.670
  282.2 5.8 rev.26
  292.2 6.2 reshape.672
  302.4 6.0 rev.27
  312.6 6.2 reshape.674
  322.8 5.8 rev.28
  332.8 6.2 reshape.676
  343.1 6.0 rev.29
  353.3 6.2 reshape.678
  363.6 5.8 rev.30
  373.6 6.2 reshape.680
  383.8 6.2 rev.31
  394.2 6.2 reshape.682
  410.4 454.0 %gather_fusion.4 = bf16[131072,16]{1,0:T(8,128)(2,1)} fusion(bf16[16,1024]{0,1:T(8,128)(2,1)S(1)} %copy.164, s32[131072]{0:T(1024)S(1)} %broadcast_clamp_fusion), kind=kCustom, calls=%fused_computation.4 | custom fusion | bytes 8912896 | tf_op jit(solution)/shard_map/jit(_take)/gather | solution.py:25
  864.4 29.0 %copy.166 = bf16[8,128,128,16]{2,1,3,0:T(8,128)(2,1)} copy(bf16[8,128,128,16]{3,2,1,0:T(8,128)(2,1)} %bitcast.208) | data formatting | bytes 8388608 | tf_op jit(solution)/shard_map/jit(_take)/gather | solution.py:25
  902.7 5.4 copy.186
  912.0 5.4 copy.189
  921.4 5.5 copy.192
  930.9 5.4 copy.195
  940.2 5.4 copy.198
  949.5 5.4 copy.201
  958.9 5.4 copy.204
  968.2 5.4 copy.207
  973.9 9.7 broadcast_in_dim.155
  983.6 9.0 scatter_fusion
  992.6 9.0 scatter_fusion.1
  1001.6 9.0 scatter_fusion.2
  1010.6 9.1 scatter_fusion.3
  1019.7 9.0 scatter_fusion.4
  1028.6 8.7 scatter_fusion.5
  1037.3 8.8 scatter_fusion.6
  1046.1 8.3 scatter_fusion.7
  1054.4 12.4 fusion.52
  1068.9 44.9 %collective-permute-start.6 = (f32[4,128,2048]{2,1,0:T(8,128)}, f32[4,128,2048]{2,1,0:T(8,128)}, u32[]{:S(2)}, u32[]{:S(2)}) collective-permute-start(f32[4,128,2048]{2,1,0:T(8,128)} %get-tuple-element.128), channel_id=1, source_target_pairs={{12,0},{16,4},{20,8},{24,12},{28,16},{32,20},{36,24},{40,28},{44,3... | collective-permute-start | bytes 12582920 | tf_op jit(solution)/shard_map/ppermute | solution.py:14
  1113.8 22.0 %collective-permute-start.5 = (f32[4,128,2048]{2,1,0:T(8,128)}, f32[4,128,2048]{2,1,0:T(8,128)}, u32[]{:S(2)}, u32[]{:S(2)}) collective-permute-start(f32[4,128,2048]{2,1,0:T(8,128)} %get-tuple-element.129), channel_id=1, source_target_pairs={{8,0},{12,4},{16,8},{20,12},{24,16},{28,20},{32,24},{36,28},{40,32... | collective-permute-start | bytes 12582920 | tf_op jit(solution)/shard_map/ppermute | solution.py:14
  1157.1 10.3 add_bitcast_fusion
  1172.0 92.0 %collective-permute-done.6 = f32[4,128,2048]{2,1,0:T(8,128)} collective-permute-done((f32[4,128,2048]{2,1,0:T(8,128)}, f32[4,128,2048]{2,1,0:T(8,128)}, u32[]{:S(2)}, u32[]{:S(2)}) %collective-permute-start.6) | collective-permute-done | bytes 4194336 | tf_op jit(solution)/shard_map/ppermute | solution.py:14
  1264.1 167.9 %collective-permute-done.5 = f32[4,128,2048]{2,1,0:T(8,128)} collective-permute-done((f32[4,128,2048]{2,1,0:T(8,128)}, f32[4,128,2048]{2,1,0:T(8,128)}, u32[]{:S(2)}, u32[]{:S(2)}) %collective-permute-start.5) | collective-permute-done | bytes 4194336 | tf_op jit(solution)/shard_map/ppermute | solution.py:14
  1432.0 10.4 fusion.5
  1442.4 6.6 reduce_sum.99
  (193 shorter events, 224.6 us)
Async XLA Ops:
  7.2 23.9 %copy-start.12 = (bf16[4,128,2048]{2,1,0:T(8,128)(2,1)S(1)}, bf16[4,128,2048]{2,1,0:T(8,128)(2,1)}, u32[]{:S(2)}) copy-start(bf16[4,128,2048]{2,1,0:T(8,128)(2,1)} %param.24) | copy-start | bytes 6291460
  7.2 1435.2 %all-gather.3.cloned.1.call-start = ((), (), s32[]{:S(2)}) async-start(), calls=%async_computation | async-start | bytes 16842752 | tf_op jit(solution)/shard_map/all_gather | solution.py:107
  7.2 47.1 %collective-permute-start = (bf16[4,128,2048]{2,1,0:T(8,128)(2,1)}, bf16[4,128,2048]{2,1,0:T(8,128)(2,1)}, u32[]{:S(2)}, u32[]{:S(2)}) collective-permute-start(bf16[4,128,2048]{2,1,0:T(8,128)(2,1)} %param.22), channel_id=1, source_target_pairs={{0,4},{4,8},{8,12},{12,16},{16,20},{20,24},{24,28},{28,32},{32,36}... | collective-permute-start | bytes 6291464 | tf_op jit(solution)/shard_map/ppermute | solution.py:14
  11.1 158.2 %collective-permute-start.1 = (bf16[4,128,2048]{2,1,0:T(8,128)(2,1)}, bf16[4,128,2048]{2,1,0:T(8,128)(2,1)}, u32[]{:S(2)}, u32[]{:S(2)}) collective-permute-start(bf16[4,128,2048]{2,1,0:T(8,128)(2,1)} %param.22), channel_id=1, source_target_pairs={{0,8},{4,12},{8,16},{12,20},{16,24},{20,28},{24,32},{28,36},{32,40... | collective-permute-start | bytes 6291464 | tf_op jit(solution)/shard_map/ppermute | solution.py:14
  14.3 160.1 %collective-permute-start.2 = (bf16[4,128,2048]{2,1,0:T(8,128)(2,1)}, bf16[4,128,2048]{2,1,0:T(8,128)(2,1)}, u32[]{:S(2)}, u32[]{:S(2)}) collective-permute-start(bf16[4,128,2048]{2,1,0:T(8,128)(2,1)} %param.22), channel_id=1, source_target_pairs={{0,12},{4,16},{8,20},{12,24},{16,28},{20,32},{24,36},{28,40},{32,4... | collective-permute-start | bytes 6291464 | tf_op jit(solution)/shard_map/ppermute | solution.py:14
  17.9 159.8 %collective-permute-start.3 = (bf16[4,128,2048]{2,1,0:T(8,128)(2,1)}, bf16[4,128,2048]{2,1,0:T(8,128)(2,1)}, u32[]{:S(2)}, u32[]{:S(2)}) collective-permute-start(bf16[4,128,2048]{2,1,0:T(8,128)(2,1)} %param.22), channel_id=1, source_target_pairs={{0,16},{4,20},{8,24},{12,28},{16,32},{20,36},{24,40},{28,44},{32,4... | collective-permute-start | bytes 6291464 | tf_op jit(solution)/shard_map/ppermute | solution.py:14
  30.5 0.6 copy-start.14
  33.5 9.5 copy-start.13
  37.6 7.0 copy-start.2
  37.6 7.0 copy-start.11
  394.2 15.6 %copy-start.16 = (f32[16,1024]{1,0:T(8,128)S(1)}, f32[16,1024]{1,0:T(8,128)}, u32[]{:S(2)}) copy-start(f32[16,1024]{1,0:T(8,128)} %param.25) | copy-start | bytes 196612
  968.2 5.4 copy-start.15
  1054.4 84.0 %copy-start = (bf16[16,8,128,128]{3,2,0,1:T(8,128)(2,1)S(1)}, bf16[16,8,128,128]{3,2,0,1:T(8,128)(2,1)}, u32[]{:S(2)}) copy-start(bf16[16,8,128,128]{3,2,0,1:T(8,128)(2,1)} %select_bitcast_fusion) | copy-start | bytes 12582916
  1054.4 84.0 %copy-start.4 = (bf16[4,1,128,2048]{2,3,0,1:T(8,128)(2,1)S(1)}, bf16[4,1,128,2048]{2,3,0,1:T(8,128)(2,1)}, u32[]{:S(2)}) copy-start(bf16[4,1,128,2048]{2,3,0,1:T(8,128)(2,1)} %copy.178) | copy-start | bytes 6291460
  1066.8 74.3 %copy-start.5 = (bf16[4,1,128,2048]{2,3,0,1:T(8,128)(2,1)S(1)}, bf16[4,1,128,2048]{2,3,0,1:T(8,128)(2,1)}, u32[]{:S(2)}) copy-start(bf16[4,1,128,2048]{2,3,0,1:T(8,128)(2,1)} %copy.176) | copy-start | bytes 6291460
  1066.8 105.2 %collective-permute-start.7 = (f32[4,128,2048]{2,1,0:T(8,128)}, f32[4,128,2048]{2,1,0:T(8,128)}, u32[]{:S(2)}, u32[]{:S(2)}) collective-permute-start(f32[4,128,2048]{2,1,0:T(8,128)} %get-tuple-element.127), channel_id=1, source_target_pairs={{16,0},{20,4},{24,8},{28,12},{32,16},{36,20},{40,24},{44,28},{48,3... | collective-permute-start | bytes 12582920 | tf_op jit(solution)/shard_map/ppermute | solution.py:14
  1068.9 195.2 %collective-permute-start.6 = (f32[4,128,2048]{2,1,0:T(8,128)}, f32[4,128,2048]{2,1,0:T(8,128)}, u32[]{:S(2)}, u32[]{:S(2)}) collective-permute-start(f32[4,128,2048]{2,1,0:T(8,128)} %get-tuple-element.128), channel_id=1, source_target_pairs={{12,0},{16,4},{20,8},{24,12},{28,16},{32,20},{36,24},{40,28},{44,3... | collective-permute-start | bytes 12582920 | tf_op jit(solution)/shard_map/ppermute | solution.py:14
  1113.8 318.1 %collective-permute-start.5 = (f32[4,128,2048]{2,1,0:T(8,128)}, f32[4,128,2048]{2,1,0:T(8,128)}, u32[]{:S(2)}, u32[]{:S(2)}) collective-permute-start(f32[4,128,2048]{2,1,0:T(8,128)} %get-tuple-element.129), channel_id=1, source_target_pairs={{8,0},{12,4},{16,8},{20,12},{24,16},{28,20},{32,24},{36,28},{40,32... | collective-permute-start | bytes 12582920 | tf_op jit(solution)/shard_map/ppermute | solution.py:14
  1135.8 296.2 %collective-permute-start.4 = (f32[4,128,2048]{2,1,0:T(8,128)}, f32[4,128,2048]{2,1,0:T(8,128)}, u32[]{:S(2)}, u32[]{:S(2)}) collective-permute-start(f32[4,128,2048]{2,1,0:T(8,128)} %get-tuple-element.126), channel_id=1, source_target_pairs={{4,0},{8,4},{12,8},{16,12},{20,16},{24,20},{28,24},{32,28},{36,32}... | collective-permute-start | bytes 12582920 | tf_op jit(solution)/shard_map/ppermute | solution.py:14
  1141.1 2.7 copy-start.6
  1143.8 2.7 copy-start.7
  1146.4 2.7 copy-start.8
  1149.1 2.6 copy-start.9
  1151.8 2.7 copy-start.10
  1154.4 2.7 copy-start.1
  1167.4 1.6 copy-start.3
Sparse Core Ops, SparseCore 0:
  410.0 186.3 all-gather.2
